TPU v7x, 32 devices: a whole 2x2x4 slice. The times are simulated.
32 devices in a mesh: node: 8 (over y, x, core), harm: 4 (over z).
Axes of the slice: x: 2, y: 2, z: 4, core: 2. Of those that a mesh axis runs over, the one named last changes fastest.
Arguments:
- krylov_basis: float32 [8, 2, 64, 16384], P(None, None, 'harm', 'node'), may hold values from -100 to 100, as said below
- cond_time: float32 [64, 16384], P('harm', 'node'), may hold values from 2 to 6
- capacity: float32 [16384], P('node'), may hold values from 0.005 to 0.05
- diag_blocks: float32 [64, 256, 256], P('node'), may hold values from -1 to 1
- coupling: float32 [64, 2, 256, 256], P('node'), may hold values from -0.375 to 0.375
- neighbours: int32 [64, 2], P('node'), may hold values from 0 to 63, as said below
- pattern: int32 [64, 2], P('node'), may hold values from 0 to 1
Outputs:
- new_vector: float32 [2, 64, 16384], P(None, 'harm', 'node')
- projections: float32 [2, 8], replicated
- new_norm: float32 [], replicated
Inputs may be any that keep to these rules, and one draw needn't show every extreme that they name: `neighbours`: with the blocks in groups of 8 consecutive ones, each entry lies in a group 1 to 3 groups away from its row's group; the present slots of the rows of one group name at most 2 distinct blocks of any other group. `krylov_basis`: each of the 8 vectors has mean squared entry 1 over its real and imaginary parts.
All inputs are finite; a program needn't handle non-finite values.
Results may differ from a plain program's by a relative error of at most 0.0003.
Values sent between devices are 32-bit elements; how exact they have to be, the bound alone decides.
A program may use at most 64 MiB of HBM per device.

v0:
```python
import functools
import math

import jax
import jax.numpy as jnp
import numpy as np
from jax import lax
from jax.experimental import pallas as pl
from jax.experimental.pallas import tpu as pltpu
from jax.sharding import PartitionSpec as P

NS_ITERS = 4
REACH = 3
USED = 2
OFFSETS = tuple(o for o in range(-REACH, REACH + 1) if o != 0)
MESH = pl.DeviceIdType.MESH
NN = (((1,), (0,)), ((), ()))
NT = (((1,), (1,)), ((), ()))


def split(x):
    high = x.astype(jnp.bfloat16)
    low = (x - high.astype(jnp.float32)).astype(jnp.bfloat16)
    return high, low


def mm(x, weights, dims):
    xh, xl = x
    wh, wl = weights
    rows = xh.shape[0]
    dot = functools.partial(
        lax.dot_general, dimension_numbers=dims, preferred_element_type=jnp.float32
    )
    both = dot(jnp.concatenate([xh, xl], axis=0), wh)
    return both[:rows] + (both[rows:] + dot(xh, wl))


def spectral_tables(count, parts):
    steps = np.arange(count)
    angles = (steps[:, None] * steps[None, :] % count) * (2.0 * math.pi / count)
    cosine = np.cos(angles) / math.sqrt(count)
    sine = np.sin(angles) / math.sqrt(count)
    table = np.block([[cosine, -sine], [sine, cosine]])
    own = count // parts
    ordered = table.reshape(2 * count, 2, parts, own).transpose(0, 2, 1, 3).reshape(2 * count, -1)
    tables = np.stack([ordered, ordered.T]).astype(np.float32)
    high = tables.astype(jnp.bfloat16)
    low = (tables - high.astype(np.float32)).astype(jnp.bfloat16)
    return np.stack([high, low], axis=1)


def kernel(
    nodes, harms,
    where_ref, request_ref, tables_ref, capacity_ref, basis_hbm, cond_hbm, diag_hbm, coupling_hbm,
    new_ref, proj_ref, norm_ref,
    basis, cond, diag, coupling, sums, wanted, cond_cols, esplit, e2split, e4split,
    solved, columns, packed, received, spectra_cols, spectra, image,
    part_node, part_harm, square_node, square_harm,
    load_sem, send_sem, recv_sem,
):
    node = lax.axis_index("node")
    harm = lax.axis_index("harm")
    kry, _, own, width = basis.shape
    blocks, bs, _ = diag.shape
    rows = 2 * own
    period = own * harms
    piece = width // harms
    last = kry - 1

    loads = [
        pltpu.make_async_copy(cond_hbm, cond, load_sem.at[0]),
        pltpu.make_async_copy(diag_hbm, diag, load_sem.at[1]),
        pltpu.make_async_copy(basis_hbm, basis, load_sem.at[2]),
        pltpu.make_async_copy(coupling_hbm, coupling, load_sem.at[3]),
    ]
    for load in loads:
        load.start()

    barrier = pltpu.get_barrier_semaphore()
    for step in range(1, harms):
        pl.semaphore_signal(
            barrier, inc=1, device_id={"harm": lax.rem(harm + step, harms)}, device_id_type=MESH
        )
    for step in range(1, nodes):
        pl.semaphore_signal(
            barrier, inc=1, device_id={"node": lax.rem(node + step, nodes)}, device_id_type=MESH
        )
    pl.semaphore_wait(barrier, harms - 1 + nodes - 1)

    counter = [0]

    def reserve(count):
        first = counter[0]
        counter[0] += count
        return first

    def around(axis, count, source, target):
        me = harm if axis == "harm" else node
        first = reserve(count)
        copies = []
        for step in range(1, count):
            peer = lax.rem(me + step, count)
            copies.append(
                pltpu.make_async_remote_copy(
                    src_ref=source(peer),
                    dst_ref=target,
                    send_sem=send_sem.at[first + step],
                    recv_sem=recv_sem.at[first + step],
                    device_id={axis: peer},
                    device_id_type=MESH,
                )
            )
            copies[-1].start()
        return copies

    def finish(copies):
        for copy in copies:
            copy.wait()

    def neighbour_copies(source, target):
        first = reserve(len(OFFSETS))
        out = []
        for at, offset in enumerate(OFFSETS):
            peer = node + offset
            copy = pltpu.make_async_remote_copy(
                src_ref=source.at[at],
                dst_ref=target.at[len(OFFSETS) - 1 - at],
                send_sem=send_sem.at[first + at],
                recv_sem=recv_sem.at[first + at],
                device_id={"node": jnp.clip(peer, 0, nodes - 1)},
                device_id_type=MESH,
            )
            sends = jnp.logical_and(peer >= 0, peer < nodes)
            back = node - offset
            receives = jnp.logical_and(back >= 0, back < nodes)
            pl.when(sends)(copy.start)
            out.append((copy, sends, receives))
        return out

    def neighbour_finish(copies):
        for copy, sends, receives in copies:
            pl.when(sends)(copy.wait_send)
            pl.when(receives)(copy.wait_recv)

    loads[0].wait()
    sums[harm] = jnp.sum(cond[...], axis=0, keepdims=True)
    sum_copies = around("harm", harms, lambda peer: sums.at[harm], sums.at[harm])
    request_copies = neighbour_copies(request_ref, wanted)
    cond_copies = around(
        "harm", harms,
        lambda peer: cond.at[:, pl.ds(pl.multiple_of(peer * piece, 128), piece)],
        cond_cols.at[harm],
    )
    mine = pl.ds(pl.multiple_of(harm * piece, 128), piece)
    cond_cols[harm] = cond[:, mine]
    received[len(OFFSETS), 0] = jnp.zeros((rows, bs), jnp.float32)
    loads[1].wait()
    loads[2].wait()
    finish(sum_copies)
    total = sums[0]
    for at in range(1, harms):
        total = total + sums[at]
    means = total / period
    inverse_means = 1.0 / means
    norm_means = means

    together = 2
    sums[harm] = means

    def lanes(b):
        return pl.ds(pl.multiple_of(b * bs, 128), bs)

    def solve(i, carry):
        ids = [i * together + k for k in range(together)]
        scale = []
        for b in ids:
            local = sums[harm, :, lanes(b)]
            scale.append(1.0 / local)
        e1 = [split(-diag[b] * s) for b, s in zip(ids, scale)]
        for b, e in zip(ids, e1):
            esplit[b, 0] = e[0]
            esplit[b, 1] = e[1]
        e2 = [split(mm(e, e, NN)) for e in e1]
        e4 = [split(mm(e, e, NN)) for e in e2]
        w = [basis[last, :, :, lanes(b)].reshape(rows, bs) for b in ids]
        for power in (e1, e2, e4):
            w = [x + mm(split(x), e, NT) for x, e in zip(w, power)]
        y = [mm(split(x), e, NT) for x, e in zip(w, e4)]
        y = [mm(split(x), e, NT) for x, e in zip(y, e4)]
        for b, x, z, s in zip(ids, w, y, scale):
            solved[:, :, lanes(b)] = ((x + z) * s).reshape(2, own, bs)
        return carry

    lax.fori_loop(0, blocks // together, solve, 0)

    column_copies = around(
        "harm", harms,
        lambda peer: solved.at[:, :, pl.ds(pl.multiple_of(peer * piece, 128), piece)],
        columns.at[harm],
    )
    columns[harm] = solved[:, :, mine]
    neighbour_finish(request_copies)
    for at in range(len(OFFSETS)):
        for slot in range(USED):
            chosen = jnp.zeros((rows, bs), jnp.float32)
            for b in range(blocks):
                line = slot * blocks + b
                flag = jnp.concatenate([wanted[at, line : line + 1, :]] * (bs // 128), axis=1)
                value = solved[:, :, b * bs : (b + 1) * bs].reshape(rows, bs)
                chosen = jnp.where(flag > 0.5, value, chosen)
            packed[at, slot] = chosen
    block_copies = neighbour_copies(packed, received)

    def direct(i, carry):
        for k in range(together):
            b = i * together + k
            local = sums[harm, :, lanes(b)]
            here = solved[:, :, lanes(b)]
            weights = (esplit[b, 0], esplit[b, 1])
            out = mm(split(here.reshape(rows, bs) * local), weights, NT).reshape(2, own, bs)
            k_at = harm * own + lax.broadcasted_iota(jnp.int32, (own, bs), 0)
            omega = (lax.rem(k_at + period // 2, period) - period // 2).astype(jnp.float32)
            react = omega * capacity_ref[:, lanes(b)]
            image[0, :, lanes(b)] = -out[0] - react * here[1]
            image[1, :, lanes(b)] = -out[1] + react * here[0]
        return carry

    lax.fori_loop(0, blocks // together, direct, 0)

    finish(cond_copies)
    finish(column_copies)
    field = columns[...].reshape(2 * period, piece)
    def table_apply(which, field):
        th = tables_ref[which, 0]
        tl = tables_ref[which, 1]
        return mm((th, tl), split(field), NN)
    samples = table_apply(0, field).reshape(2, period, piece)
    driven = samples * cond_cols[...].reshape(period, piece)[None]
    spectra_cols[...] = table_apply(1, driven.reshape(2 * period, piece)).reshape(
        harms, 2, own, piece
    )
    spectra_copies = around("harm", harms, lambda peer: spectra_cols.at[peer], spectra.at[harm])
    spectra[harm] = spectra_cols[harm]

    loads[3].wait()
    neighbour_finish(block_copies)

    def couple(b, carry):
        out = image[:, :, lanes(b)].reshape(rows, bs)
        for slot in range(coupling.shape[1]):
            line = where_ref[b, slot]
            picked = received[line // USED, lax.rem(line, USED)]
            out = out + mm(split(picked), split(coupling[b, slot]), NT)
        image[:, :, lanes(b)] = out.reshape(2, own, bs)
        return carry

    lax.fori_loop(0, blocks, couple, 0, unroll=2)
    finish(spectra_copies)

    for at in range(harms):
        area = pl.ds(at * piece, piece)
        image[:, :, area] = image[:, :, area] + spectra[at]

    def fold(x):
        x = x.reshape(own // 8, 8, x.shape[1]).sum(0)
        out = x[:, 0:128]
        for at in range(1, x.shape[1] // 128):
            out = out + x[:, at * 128 : (at + 1) * 128]
        return jnp.sum(out, axis=0, keepdims=True)

    def exchange(parts_node, parts_harm):
        finish(around("node", nodes, lambda peer: parts_node.at[node], parts_node.at[node]))
        value = parts_node[0]
        for at in range(1, nodes):
            value = value + parts_node[at]
        parts_harm[harm] = value
        finish(around("harm", harms, lambda peer: parts_harm.at[harm], parts_harm.at[harm]))
        value = parts_harm[0]
        for at in range(1, harms):
            value = value + parts_harm[at]
        return jnp.sum(value, axis=1, keepdims=True)

    count = float(period * width * nodes)
    for m in range(kry):
        br, bi = basis[m, 0], basis[m, 1]
        part_node[node, m : m + 1] = fold(br * image[0] + bi * image[1])
        part_node[node, kry + m : kry + m + 1] = fold(br * image[1] - bi * image[0])
    proj = exchange(part_node, part_harm) / count
    proj_ref[...] = jnp.broadcast_to(proj, proj_ref.shape)

    squares = jnp.zeros((1, 128), jnp.float32)
    tile = 512
    for at in range(0, width, tile):
        area = slice(at, at + tile)
        real, imag = image[0, :, area], image[1, :, area]
        for m in range(kry):
            pr = jnp.broadcast_to(proj[m : m + 1], (own, tile))
            pi = jnp.broadcast_to(proj[kry + m : kry + m + 1], (own, tile))
            br, bi = basis[m, 0, :, area], basis[m, 1, :, area]
            real = real - (pr * br - pi * bi)
            imag = imag - (pr * bi + pi * br)
        image[0, :, area] = real
        image[1, :, area] = imag
        squares = squares + fold(real * real + imag * imag)
    square_node[node] = jnp.concatenate([squares, jnp.zeros((7, 128), jnp.float32)], axis=0)
    square = exchange(square_node, square_harm)[0:1] / count
    norm = jnp.sqrt(square + 1e-6)
    norm_ref[...] = jnp.broadcast_to(norm, norm_ref.shape)
    inverse_norm = 1.0 / norm
    for p in range(2):
        new_ref[p] = image[p] * jnp.broadcast_to(inverse_norm, (own, width))


def coupling_tables(neighbours, pattern, blocks):
    node = lax.axis_index("node")
    flat = neighbours.reshape(-1)
    present = pattern.reshape(-1) != 0
    offset = flat // blocks - node
    at = jnp.where(offset < 0, offset + REACH, offset + REACH - 1)
    block = flat % blocks
    kinds = jnp.arange(len(OFFSETS))
    numbers = jnp.arange(blocks)
    hits = (
        present[:, None, None]
        & (at[:, None, None] == kinds[None, :, None])
        & (block[:, None, None] == numbers[None, None, :])
    )
    used = jnp.any(hits, axis=0)
    before = jnp.sum(used[:, None, :] & (numbers[None, None, :] < numbers[None, :, None]), axis=2)
    slots = jnp.arange(USED)
    flags = used[:, None, :] & (before[:, None, :] == slots[None, :, None])
    request = jnp.broadcast_to(
        flags.reshape(len(OFFSETS), USED * blocks, 1).astype(jnp.float32),
        (len(OFFSETS), USED * blocks, 128),
    )
    slot = jnp.sum(jnp.where(hits, before[None], 0), axis=(1, 2))
    where = jnp.where(present, at * USED + slot, len(OFFSETS) * USED)
    where = jnp.clip(where, 0, len(OFFSETS) * USED)
    return where.reshape(neighbours.shape).astype(jnp.int32), request


def per_device(nodes, harms, krylov_basis, cond_time, capacity, diag_blocks, coupling, neighbours, pattern):
    kry, _, own, width = krylov_basis.shape
    blocks, bs, _ = diag_blocks.shape
    period = own * harms
    piece = width // harms
    rows = 2 * own
    where, request = coupling_tables(neighbours, pattern, blocks)
    tables = jnp.asarray(spectral_tables(period, harms))
    kinds = len(OFFSETS)
    sems = 5 * harms + 2 * kinds + 2 * nodes + 2 * harms
    f32, bf16 = jnp.float32, jnp.bfloat16
    vmem = pl.BlockSpec(memory_space=pltpu.VMEM)
    hbm = pl.BlockSpec(memory_space=pl.ANY)
    new, proj, norm = pl.pallas_call(
        functools.partial(kernel, nodes, harms),
        out_shape=(
            jax.ShapeDtypeStruct((2, own, width), f32),
            jax.ShapeDtypeStruct((2 * kry, 128), f32),
            jax.ShapeDtypeStruct((8, 128), f32),
        ),
        in_specs=[pl.BlockSpec(memory_space=pltpu.SMEM), vmem, vmem, vmem, hbm, hbm, hbm, hbm],
        out_specs=(vmem, vmem, vmem),
        scratch_shapes=[
            pltpu.VMEM(krylov_basis.shape, f32),
            pltpu.VMEM(cond_time.shape, f32),
            pltpu.VMEM(diag_blocks.shape, f32),
            pltpu.VMEM(coupling.shape, f32),
            pltpu.VMEM((harms, 1, width), f32),
            pltpu.VMEM((kinds, USED * blocks, 128), f32),
            pltpu.VMEM((harms, own, piece), f32),
            pltpu.VMEM((blocks, 2, bs, bs), bf16),
            pltpu.VMEM((1, 2, bs, bs), bf16),
            pltpu.VMEM((1, 2, bs, bs), bf16),
            pltpu.VMEM((2, own, width), f32),
            pltpu.VMEM((harms, 2, own, piece), f32),
            pltpu.VMEM((kinds, USED, rows, bs), f32),
            pltpu.VMEM((kinds + 1, USED, rows, bs), f32),
            pltpu.VMEM((harms, 2, own, piece), f32),
            pltpu.VMEM((harms, 2, own, piece), f32),
            pltpu.VMEM((2, own, width), f32),
            pltpu.VMEM((nodes, 2 * kry, 128), f32),
            pltpu.VMEM((harms, 2 * kry, 128), f32),
            pltpu.VMEM((nodes, 8, 128), f32),
            pltpu.VMEM((harms, 8, 128), f32),
            pltpu.SemaphoreType.DMA((4,)),
            pltpu.SemaphoreType.DMA((sems,)),
            pltpu.SemaphoreType.DMA((sems,)),
        ],
        compiler_params=pltpu.CompilerParams(
            collective_id=0, has_side_effects=True, vmem_limit_bytes=60 * 1024 * 1024
        ),
        name="arnoldi_step",
    )(where, request, tables, capacity.reshape(1, width), krylov_basis, cond_time, diag_blocks, coupling)
    return new, proj[:, 0].reshape(2, kry), norm[0, 0]


def solution(mesh):
    shape = dict(mesh.shape)
    return jax.shard_map(
        functools.partial(per_device, shape["node"], shape["harm"]),
        mesh=mesh,
        in_specs=(
            P(None, None, "harm", "node"),
            P("harm", "node"),
            P("node"),
            P("node", None, None),
            P("node", None, None, None),
            P("node", None),
            P("node", None),
        ),
        out_specs=(P(None, "harm", "node"), P(), P()),
        check_vma=False,
    )
```

profile of v0, /device:TPU:0, one launch (start us, length us, event | category | flops | bytes accessed | tf_op | source)
XLA Modules:
  0.0 54.5 jit_solution(10054293360928178870)
XLA Ops:
  0.7 0.1 eq.71
  0.7 0.8 %copy.39 = s32[8,2]{1,0:T(8,128)S(1)} copy(s32[8,2]{0,1:T(2,128)} %param.13) | data formatting | bytes 128 | tf_op args[5]
  1.5 0.1 reshape.188
  1.6 0.8 %copy.38 = s32[8,2]{1,0:T(8,128)S(1)} copy(s32[8,2]{0,1:T(2,128)} %param.14) | data formatting | bytes 128 | tf_op args[6]
  2.4 0.1 ne.57
  2.5 0.2 and_reduce_fusion
  2.7 0.1 copy.44
  2.8 0.1 copy.45
  2.9 0.2 convert_reduce_fusion
  3.1 0.1 fusion
  3.2 0.1 eq.69
  3.2 0.1 reduce_sum.22
  3.3 0.6 %select_clamp_fusion.where_ref = s32[8,2]{1,0:T(8,128)} fusion(s32[8,2]{1,0:T(8,128)S(1)} %reduce_sum.22, s32[8,2]{1,0:T(8,128)S(1)} %copy.39, s32[]{:T(128)S(6)} %axis_index.15, s32[8,2]{1,0:T(8,128)S(1)} %copy.38), kind=kLoop, calls=%fused_computation.11 | loop fusion | flops 400 | bytes 260 | tf_op jit(solution)/shard_map/jit(clip)/min | solution.py:338
  3.9 0.7 %broadcast_in_dim.13.request_ref = f32[6,16,128]{2,1,0:T(8,128)} broadcast(f32[6,16]{1,0:T(8,128)S(1)} %and_convert_fusion), dimensions={0,1} | broadcast | bytes 49536 | tf_op jit(solution)/shard_map/broadcast_in_dim | solution.py:332
  4.6 45.6 %arnoldi_step.1 = (f32[2,16,2048]{2,1,0:T(8,128)}, f32[16,128]{1,0:T(8,128)}, f32[8,128]{1,0:T(8,128)}) custom-call(s32[8,2]{1,0:T(8,128)} %select_clamp_fusion.where_ref, f32[6,16,128]{2,1,0:T(8,128)} %broadcast_in_dim.13.request_ref, bf16[2,2,128,128]{3,2,1,0:T(8,128)(2,1)} %constant.49.clone.tables_ref, f32[1,2048]{1,0:T(1,128)} %bitcast.4, ...), custom_call_target="tpu_custom_call" | custom-call | tf_op jit(solution)/shard_map/arnoldi_step/pallas_call | solution.py:355
  50.2 1.2 %slice.7 = f32[1,1]{1,0:T(1,128)} slice(f32[8,128]{1,0:T(8,128)} %get-tuple-element.8), slice={[0:1], [0:1]} | slice | bytes 8 | tf_op jit(solution)/shard_map/slice | solution.py:395
  51.4 0.8 %slice_reduce_fusion = f32[16]{0:T(128)S(1)} fusion(f32[16,128]{1,0:T(8,128)} %get-tuple-element.7), kind=kLoop, calls=%fused_computation.4 | loop fusion | bytes 128 | tf_op jit(solution)/shard_map/slice | solution.py:395
  52.2 0.6 %reshape_squeeze.3 = f32[2,8]{1,0:T(2,128)} reshape(f32[16]{0:T(128)S(1)} %slice_reduce_fusion) | data formatting | bytes 128 | tf_op jit(solution)/shard_map/reshape;squeeze | solution.py:395
  52.9 1.7 %copy.47 = f32[2,16,2048]{2,1,0:T(8,128)} copy(f32[2,16,2048]{2,1,0:T(8,128)} %get-tuple-element.14) | data formatting | bytes 524288
  (9 shorter events, 0.1 us)
where the time goes:
time: 54.8 us; the launch traced here: 54.5 us
  Pallas kernels  45.6 us (83%)
  local copies, waits for them, and re-layouts  7.14 us (13%)
  other arithmetic  1.14 us (2%)
  between operations  0.68 us (1%)
    pallas_call x1, Pallas kernels, per_device(): pl.pallas_call(functools.partial(kernel, nodes, harms), out_shape=(jax.Sh...  45.6 us
    unnamed x3, local copies, waits for them, and re-layouts  3.18 us
    slice x2, local copies, waits for them, and re-layouts, per_device(): return (new, proj[:, 0].reshape(2, kry), norm[0, 0])  2 us

commit v1 on v0

--- a/solution.py
+++ b/solution.py
@@ -51,9 +51,9 @@
 
 def kernel(
     nodes, harms,
-    where_ref, request_ref, tables_ref, capacity_ref, basis_hbm, cond_hbm, diag_hbm, coupling_hbm,
+    near_ref, pattern_ref, tables_ref, capacity_ref, basis_hbm, cond_hbm, diag_hbm, coupling_hbm,
     new_ref, proj_ref, norm_ref,
-    basis, cond, diag, coupling, sums, wanted, cond_cols, esplit, e2split, e4split,
+    basis, cond, diag, coupling, sums, wanted, cond_cols, esplit, where_ref, request,
     solved, columns, packed, received, spectra_cols, spectra, image,
     part_node, part_harm, square_node, square_harm,
     load_sem, send_sem, recv_sem,
@@ -70,8 +70,9 @@
     loads = [
         pltpu.make_async_copy(cond_hbm, cond, load_sem.at[0]),
         pltpu.make_async_copy(diag_hbm, diag, load_sem.at[1]),
-        pltpu.make_async_copy(basis_hbm, basis, load_sem.at[2]),
+        pltpu.make_async_copy(basis_hbm.at[last], basis.at[last], load_sem.at[2]),
         pltpu.make_async_copy(coupling_hbm, coupling, load_sem.at[3]),
+        pltpu.make_async_copy(basis_hbm.at[0:last], basis.at[0:last], load_sem.at[4]),
     ]
     for load in loads:
         load.start()
@@ -85,6 +86,10 @@
         pl.semaphore_signal(
             barrier, inc=1, device_id={"node": lax.rem(node + step, nodes)}, device_id_type=MESH
         )
+    coupling_tables(node, near_ref, pattern_ref, where_ref, request)
+    received[len(OFFSETS), 0] = jnp.zeros((rows, bs), jnp.float32)
+    loads[0].wait()
+    sums[harm] = jnp.sum(cond[...], axis=0, keepdims=True)
     pl.semaphore_wait(barrier, harms - 1 + nodes - 1)
 
     counter = [0]
@@ -142,10 +147,8 @@
             pl.when(sends)(copy.wait_send)
             pl.when(receives)(copy.wait_recv)
 
-    loads[0].wait()
-    sums[harm] = jnp.sum(cond[...], axis=0, keepdims=True)
     sum_copies = around("harm", harms, lambda peer: sums.at[harm], sums.at[harm])
-    request_copies = neighbour_copies(request_ref, wanted)
+    request_copies = neighbour_copies(request, wanted)
     cond_copies = around(
         "harm", harms,
         lambda peer: cond.at[:, pl.ds(pl.multiple_of(peer * piece, 128), piece)],
@@ -153,7 +156,6 @@
     )
     mine = pl.ds(pl.multiple_of(harm * piece, 128), piece)
     cond_cols[harm] = cond[:, mine]
-    received[len(OFFSETS), 0] = jnp.zeros((rows, bs), jnp.float32)
     loads[1].wait()
     loads[2].wait()
     finish(sum_copies)
@@ -161,8 +163,6 @@
     for at in range(1, harms):
         total = total + sums[at]
     means = total / period
-    inverse_means = 1.0 / means
-    norm_means = means
 
     together = 2
     sums[harm] = means
@@ -170,12 +170,8 @@
     def lanes(b):
         return pl.ds(pl.multiple_of(b * bs, 128), bs)
 
-    def solve(i, carry):
-        ids = [i * together + k for k in range(together)]
-        scale = []
-        for b in ids:
-            local = sums[harm, :, lanes(b)]
-            scale.append(1.0 / local)
+    def solve(ids):
+        scale = [1.0 / sums[harm, :, lanes(b)] for b in ids]
         e1 = [split(-diag[b] * s) for b, s in zip(ids, scale)]
         for b, e in zip(ids, e1):
             esplit[b, 0] = e[0]
@@ -189,15 +185,24 @@
         y = [mm(split(x), e, NT) for x, e in zip(y, e4)]
         for b, x, z, s in zip(ids, w, y, scale):
             solved[:, :, lanes(b)] = ((x + z) * s).reshape(2, own, bs)
-        return carry
-
-    lax.fori_loop(0, blocks // together, solve, 0)
-
-    column_copies = around(
-        "harm", harms,
-        lambda peer: solved.at[:, :, pl.ds(pl.multiple_of(peer * piece, 128), piece)],
-        columns.at[harm],
-    )
+
+    first_column = reserve(harms)
+    column_copies = []
+    per_piece = piece // bs
+    for step in range(1, harms + 1):
+        peer = lax.rem(harm + step, harms)
+        solve([peer * per_piece + k for k in range(per_piece)])
+        if step < harms:
+            copy = pltpu.make_async_remote_copy(
+                src_ref=solved.at[:, :, pl.ds(pl.multiple_of(peer * piece, 128), piece)],
+                dst_ref=columns.at[harm],
+                send_sem=send_sem.at[first_column + step],
+                recv_sem=recv_sem.at[first_column + step],
+                device_id={"harm": peer},
+                device_id_type=MESH,
+            )
+            copy.start()
+            column_copies.append(copy)
     columns[harm] = solved[:, :, mine]
     neighbour_finish(request_copies)
     for at in range(len(OFFSETS)):
@@ -257,6 +262,7 @@
     lax.fori_loop(0, blocks, couple, 0, unroll=2)
     finish(spectra_copies)
 
+    loads[4].wait()
     for at in range(harms):
         area = pl.ds(at * piece, piece)
         image[:, :, area] = image[:, :, area] + spectra[at]
@@ -286,7 +292,11 @@
         part_node[node, m : m + 1] = fold(br * image[0] + bi * image[1])
         part_node[node, kry + m : kry + m + 1] = fold(br * image[1] - bi * image[0])
     proj = exchange(part_node, part_harm) / count
-    proj_ref[...] = jnp.broadcast_to(proj, proj_ref.shape)
+    row_at = lax.broadcasted_iota(jnp.int32, (2 * kry, 128), 0)
+    lane_at = lax.broadcasted_iota(jnp.int32, (2 * kry, 128), 1)
+    for p in range(2):
+        line = jnp.where(row_at == lane_at + p * kry, jnp.broadcast_to(proj, row_at.shape), 0.0)
+        proj_ref[p : p + 1, :] = jnp.sum(line, axis=0, keepdims=True)[:, 0:kry]
 
     squares = jnp.zeros((1, 128), jnp.float32)
     tile = 512
@@ -299,44 +309,40 @@
             br, bi = basis[m, 0, :, area], basis[m, 1, :, area]
             real = real - (pr * br - pi * bi)
             imag = imag - (pr * bi + pi * br)
-        image[0, :, area] = real
-        image[1, :, area] = imag
+        new_ref[0, :, area] = real
+        new_ref[1, :, area] = imag
         squares = squares + fold(real * real + imag * imag)
     square_node[node] = jnp.concatenate([squares, jnp.zeros((7, 128), jnp.float32)], axis=0)
     square = exchange(square_node, square_harm)[0:1] / count
-    norm = jnp.sqrt(square + 1e-6)
-    norm_ref[...] = jnp.broadcast_to(norm, norm_ref.shape)
-    inverse_norm = 1.0 / norm
-    for p in range(2):
-        new_ref[p] = image[p] * jnp.broadcast_to(inverse_norm, (own, width))
-
-
-def coupling_tables(neighbours, pattern, blocks):
-    node = lax.axis_index("node")
-    flat = neighbours.reshape(-1)
-    present = pattern.reshape(-1) != 0
-    offset = flat // blocks - node
-    at = jnp.where(offset < 0, offset + REACH, offset + REACH - 1)
-    block = flat % blocks
-    kinds = jnp.arange(len(OFFSETS))
-    numbers = jnp.arange(blocks)
-    hits = (
-        present[:, None, None]
-        & (at[:, None, None] == kinds[None, :, None])
-        & (block[:, None, None] == numbers[None, None, :])
-    )
-    used = jnp.any(hits, axis=0)
-    before = jnp.sum(used[:, None, :] & (numbers[None, None, :] < numbers[None, :, None]), axis=2)
-    slots = jnp.arange(USED)
-    flags = used[:, None, :] & (before[:, None, :] == slots[None, :, None])
-    request = jnp.broadcast_to(
-        flags.reshape(len(OFFSETS), USED * blocks, 1).astype(jnp.float32),
-        (len(OFFSETS), USED * blocks, 128),
-    )
-    slot = jnp.sum(jnp.where(hits, before[None], 0), axis=(1, 2))
-    where = jnp.where(present, at * USED + slot, len(OFFSETS) * USED)
-    where = jnp.clip(where, 0, len(OFFSETS) * USED)
-    return where.reshape(neighbours.shape).astype(jnp.int32), request
+    norm_ref[...] = jnp.sqrt(square + 1e-6)
+
+
+def coupling_tables(node, near_ref, pattern_ref, where_ref, request):
+    slots, blocks = near_ref.shape
+    kinds, lines, _ = request.shape
+    entries = []
+    for b in range(blocks):
+        for j in range(slots):
+            near = near_ref[j, b]
+            offset = lax.div(near, blocks) - node
+            at = jnp.where(offset < 0, offset + REACH, offset + REACH - 1)
+            present = pattern_ref[j, b] != 0
+            code = jnp.where(present, at * blocks + lax.rem(near, blocks), -1)
+            entries.append((b, j, at, present, code))
+    number = lax.broadcasted_iota(jnp.int32, (kinds * lines, 128), 0)
+    hot = jnp.zeros((kinds * lines, 128), jnp.float32)
+    for b, j, at, present, code in entries:
+        start = at * blocks
+        slot = jnp.int32(0)
+        for entry in entries:
+            other = entry[4]
+            lower = jnp.logical_and(other >= start, other < code)
+            slot = jnp.where(lower, 1, slot)
+        line = jnp.where(present, at * USED + slot, kinds * USED)
+        where_ref[b, j] = jnp.clip(line, 0, kinds * USED)
+        key = jnp.where(present, code + (at + slot) * blocks, -1)
+        hot = jnp.where(number == key, 1.0, hot)
+    request[...] = hot.reshape(request.shape)
 
 
 def per_device(nodes, harms, krylov_basis, cond_time, capacity, diag_blocks, coupling, neighbours, pattern):
@@ -345,21 +351,21 @@
     period = own * harms
     piece = width // harms
     rows = 2 * own
-    where, request = coupling_tables(neighbours, pattern, blocks)
     tables = jnp.asarray(spectral_tables(period, harms))
     kinds = len(OFFSETS)
     sems = 5 * harms + 2 * kinds + 2 * nodes + 2 * harms
     f32, bf16 = jnp.float32, jnp.bfloat16
     vmem = pl.BlockSpec(memory_space=pltpu.VMEM)
     hbm = pl.BlockSpec(memory_space=pl.ANY)
-    new, proj, norm = pl.pallas_call(
+    smem = pl.BlockSpec(memory_space=pltpu.SMEM)
+    rest, proj, norm = pl.pallas_call(
         functools.partial(kernel, nodes, harms),
         out_shape=(
             jax.ShapeDtypeStruct((2, own, width), f32),
-            jax.ShapeDtypeStruct((2 * kry, 128), f32),
-            jax.ShapeDtypeStruct((8, 128), f32),
+            jax.ShapeDtypeStruct((2, kry), f32),
+            jax.ShapeDtypeStruct((1, 1), f32),
         ),
-        in_specs=[pl.BlockSpec(memory_space=pltpu.SMEM), vmem, vmem, vmem, hbm, hbm, hbm, hbm],
+        in_specs=[smem, smem, vmem, vmem, hbm, hbm, hbm, hbm],
         out_specs=(vmem, vmem, vmem),
         scratch_shapes=[
             pltpu.VMEM(krylov_basis.shape, f32),
@@ -370,8 +376,8 @@
             pltpu.VMEM((kinds, USED * blocks, 128), f32),
             pltpu.VMEM((harms, own, piece), f32),
             pltpu.VMEM((blocks, 2, bs, bs), bf16),
-            pltpu.VMEM((1, 2, bs, bs), bf16),
-            pltpu.VMEM((1, 2, bs, bs), bf16),
+            pltpu.SMEM(neighbours.shape, jnp.int32),
+            pltpu.VMEM((kinds, USED * blocks, 128), f32),
             pltpu.VMEM((2, own, width), f32),
             pltpu.VMEM((harms, 2, own, piece), f32),
             pltpu.VMEM((kinds, USED, rows, bs), f32),
@@ -383,7 +389,7 @@
             pltpu.VMEM((harms, 2 * kry, 128), f32),
             pltpu.VMEM((nodes, 8, 128), f32),
             pltpu.VMEM((harms, 8, 128), f32),
-            pltpu.SemaphoreType.DMA((4,)),
+            pltpu.SemaphoreType.DMA((5,)),
             pltpu.SemaphoreType.DMA((sems,)),
             pltpu.SemaphoreType.DMA((sems,)),
         ],
@@ -391,8 +397,9 @@
             collective_id=0, has_side_effects=True, vmem_limit_bytes=60 * 1024 * 1024
         ),
         name="arnoldi_step",
-    )(where, request, tables, capacity.reshape(1, width), krylov_basis, cond_time, diag_blocks, coupling)
-    return new, proj[:, 0].reshape(2, kry), norm[0, 0]
+    )(neighbours.T, pattern.T, tables, capacity.reshape(1, width), krylov_basis, cond_time, diag_blocks, coupling)
+    norm = norm[0, 0]
+    return rest * (1.0 / norm), proj, norm
 
 
 def solution(mesh):

time: 54.8 us -> 47.6 us (0.87)
  local copies, waits for them, and re-layouts: 7.14 us -> 1.23 us
  Pallas kernels: 45.6 us -> 41.6 us
  between operations: 0.68 us -> 2.9 us
    pallas_call x1, Pallas kernels: 45.6 us -> 41.6 us  [per_device(): pl.pallas_call(functools.partial(kernel, nodes, harms), out_shape=(jax.Sh...]
    slice x2 -> x0, local copies, waits for them, and re-layouts: 2 us -> none  [per_device(): return (new, proj[:, 0].reshape(2, kry), norm[0, 0])]
    unnamed x3 -> x1, local copies, waits for them, and re-layouts: 3.18 us -> 1.23 us
    mul x0 -> x1, other arithmetic: none -> 1.67 us  [per_device(): return (rest * (1.0 / norm), proj, norm)]
    broadcast_in_dim x1 -> x0, local copies, waits for them, and re-layouts: 0.7 us -> none  [coupling_tables(): jnp.broadcast_to(flags.reshape(len(OFFSETS), USED * blocks, 1).astype(jnp...]
    another operation x1 -> x0, local copies, waits for them, and re-layouts: 0.65 us -> none  [per_device(): return (new, proj[:, 0].reshape(2, kry), norm[0, 0])]
    min x1 -> x0, other arithmetic: 0.62 us -> none  [coupling_tables(): where = jnp.clip(where, 0, len(OFFSETS) * USED)]
where the time goes in v1:
time: 47.6 us; the launch traced here: 47.4 us
  Pallas kernels  41.6 us (87%)
  between operations  2.9 us (6%)
  other arithmetic  1.67 us (4%)
  local copies, waits for them, and re-layouts  1.23 us (3%)
    pallas_call x1, Pallas kernels, per_device(): pl.pallas_call(functools.partial(kernel, nodes, harms), out_shape=(jax.Sh...  41.6 us
    mul x1, other arithmetic, per_device(): return (rest * (1.0 / norm), proj, norm)  1.67 us
    unnamed x1, local copies, waits for them, and re-layouts  1.23 us

profile of v1, /device:TPU:0, one launch (start us, length us, event | category | flops | bytes accessed | tf_op | source)
XLA Modules:
  0.0 47.4 jit_solution(1163026580212825889)
XLA Ops:
  0.6 41.6 %arnoldi_step.1 = (f32[2,16,2048]{2,1,0:T(8,128)}, f32[2,8]{1,0:T(2,128)}, f32[1,1]{1,0:T(1,128)}) custom-call(s32[2,8]{1,0:T(2,128)} %bitcast.5, s32[2,8]{1,0:T(2,128)} %bitcast.6, bf16[2,2,128,128]{3,2,1,0:T(8,128)(2,1)} %constant.4.clone.tables_ref, f32[1,2048]{1,0:T(1,128)} %bitcast.4, f32[8,2,16,2048]{3,2,1,0:T(8,128)} %basis_hbm.1, ...), custom_call_target="tpu_custom_call" | custom-call | tf_op jit(solution)/shard_map/arnoldi_step/pallas_call | solution.py:361
  42.8 1.7 %broadcast_multiply_fusion = f32[2,16,2048]{2,1,0:T(8,128)} fusion(f32[2,16,2048]{2,1,0:T(8,128)} %get-tuple-element.6, f32[]{:T(128)S(6)} %div.3), kind=kLoop, calls=%fused_computation | loop fusion | flops 65536 | bytes 524292 | tf_op jit(solution)/shard_map/mul | solution.py:402
  44.5 1.2 %copy.13 = f32[2,8]{1,0:T(2,128)} copy(f32[2,8]{1,0:T(2,128)} %get-tuple-element.13) | data formatting | bytes 128

commit v2 on v1

--- a/solution.py
+++ b/solution.py
@@ -55,7 +55,7 @@
     new_ref, proj_ref, norm_ref,
     basis, cond, diag, coupling, sums, wanted, cond_cols, esplit, where_ref, request,
     solved, columns, packed, received, spectra_cols, spectra, image,
-    part_node, part_harm, square_node, square_harm,
+    part_rows, square_rows,
     load_sem, send_sem, recv_sem,
 ):
     node = lax.axis_index("node")
@@ -78,19 +78,23 @@
         load.start()
 
     barrier = pltpu.get_barrier_semaphore()
-    for step in range(1, harms):
-        pl.semaphore_signal(
-            barrier, inc=1, device_id={"harm": lax.rem(harm + step, harms)}, device_id_type=MESH
-        )
-    for step in range(1, nodes):
-        pl.semaphore_signal(
-            barrier, inc=1, device_id={"node": lax.rem(node + step, nodes)}, device_id_type=MESH
-        )
+    total_devices = nodes * harms
+    flat = node * harms + harm
+
+    def device(step):
+        peer = lax.rem(flat + step, total_devices)
+        return (lax.div(peer, harms), lax.rem(peer, harms))
+
+    def greet(step, carry):
+        pl.semaphore_signal(barrier, inc=1, device_id=device(step), device_id_type=MESH)
+        return carry
+
+    lax.fori_loop(1, total_devices, greet, 0)
     coupling_tables(node, near_ref, pattern_ref, where_ref, request)
     received[len(OFFSETS), 0] = jnp.zeros((rows, bs), jnp.float32)
     loads[0].wait()
     sums[harm] = jnp.sum(cond[...], axis=0, keepdims=True)
-    pl.semaphore_wait(barrier, harms - 1 + nodes - 1)
+    pl.semaphore_wait(barrier, total_devices - 1)
 
     counter = [0]
 
@@ -274,29 +278,51 @@
             out = out + x[:, at * 128 : (at + 1) * 128]
         return jnp.sum(out, axis=0, keepdims=True)
 
-    def exchange(parts_node, parts_harm):
-        finish(around("node", nodes, lambda peer: parts_node.at[node], parts_node.at[node]))
-        value = parts_node[0]
-        for at in range(1, nodes):
-            value = value + parts_node[at]
-        parts_harm[harm] = value
-        finish(around("harm", harms, lambda peer: parts_harm.at[harm], parts_harm.at[harm]))
-        value = parts_harm[0]
-        for at in range(1, harms):
-            value = value + parts_harm[at]
-        return jnp.sum(value, axis=1, keepdims=True)
+    def exchange(parts):
+        first = reserve(total_devices)
+
+        def copy(step):
+            return pltpu.make_async_remote_copy(
+                src_ref=parts.at[flat],
+                dst_ref=parts.at[flat],
+                send_sem=send_sem.at[first + step],
+                recv_sem=recv_sem.at[first + step],
+                device_id=device(step),
+                device_id_type=MESH,
+            )
+
+        def start(step, carry):
+            copy(step).start()
+            return carry
+
+        def wait(step, carry):
+            copy(step).wait()
+            return carry
+
+        lax.fori_loop(1, total_devices, start, 0)
+        lax.fori_loop(1, total_devices, wait, 0)
+        rows = [parts[at] for at in range(total_devices)]
+        while len(rows) > 1:
+            rows = [sum(rows[at : at + 2][1:], rows[at]) for at in range(0, len(rows), 2)]
+        return rows[0]
+
+    row_at = lax.broadcasted_iota(jnp.int32, (2 * kry, 128), 0)
+    lane_at = lax.broadcasted_iota(jnp.int32, (2 * kry, 128), 1)
 
     count = float(period * width * nodes)
+    reals, imags = [], []
     for m in range(kry):
         br, bi = basis[m, 0], basis[m, 1]
-        part_node[node, m : m + 1] = fold(br * image[0] + bi * image[1])
-        part_node[node, kry + m : kry + m + 1] = fold(br * image[1] - bi * image[0])
-    proj = exchange(part_node, part_harm) / count
-    row_at = lax.broadcasted_iota(jnp.int32, (2 * kry, 128), 0)
-    lane_at = lax.broadcasted_iota(jnp.int32, (2 * kry, 128), 1)
-    for p in range(2):
-        line = jnp.where(row_at == lane_at + p * kry, jnp.broadcast_to(proj, row_at.shape), 0.0)
-        proj_ref[p : p + 1, :] = jnp.sum(line, axis=0, keepdims=True)[:, 0:kry]
+        reals.append(fold(br * image[0] + bi * image[1]))
+        imags.append(fold(br * image[1] - bi * image[0]))
+    local = jnp.sum(jnp.concatenate(reals + imags, axis=0), axis=1, keepdims=True)
+    line = jnp.where(row_at == lane_at, jnp.broadcast_to(local, row_at.shape), 0.0)
+    part_rows[flat] = jnp.sum(line, axis=0, keepdims=True)
+    found = exchange(part_rows) / count
+    line = jnp.where(row_at == lane_at, jnp.broadcast_to(found, row_at.shape), 0.0)
+    proj = jnp.sum(line, axis=1, keepdims=True)
+    proj_ref[0:1, :] = found[:, 0:kry]
+    proj_ref[1:2, :] = found[:, kry : 2 * kry]
 
     squares = jnp.zeros((1, 128), jnp.float32)
     tile = 512
@@ -312,9 +338,8 @@
         new_ref[0, :, area] = real
         new_ref[1, :, area] = imag
         squares = squares + fold(real * real + imag * imag)
-    square_node[node] = jnp.concatenate([squares, jnp.zeros((7, 128), jnp.float32)], axis=0)
-    square = exchange(square_node, square_harm)[0:1] / count
-    norm_ref[...] = jnp.sqrt(square + 1e-6)
+    square_rows[flat] = squares
+    norm_ref[...] = jnp.sum(exchange(square_rows), axis=1, keepdims=True) / count
 
 
 def coupling_tables(node, near_ref, pattern_ref, where_ref, request):
@@ -353,12 +378,12 @@
     rows = 2 * own
     tables = jnp.asarray(spectral_tables(period, harms))
     kinds = len(OFFSETS)
-    sems = 5 * harms + 2 * kinds + 2 * nodes + 2 * harms
+    sems = 4 * harms + 2 * kinds + 2 * nodes * harms
     f32, bf16 = jnp.float32, jnp.bfloat16
     vmem = pl.BlockSpec(memory_space=pltpu.VMEM)
     hbm = pl.BlockSpec(memory_space=pl.ANY)
     smem = pl.BlockSpec(memory_space=pltpu.SMEM)
-    rest, proj, norm = pl.pallas_call(
+    rest, proj, square = pl.pallas_call(
         functools.partial(kernel, nodes, harms),
         out_shape=(
             jax.ShapeDtypeStruct((2, own, width), f32),
@@ -385,10 +410,8 @@
             pltpu.VMEM((harms, 2, own, piece), f32),
             pltpu.VMEM((harms, 2, own, piece), f32),
             pltpu.VMEM((2, own, width), f32),
-            pltpu.VMEM((nodes, 2 * kry, 128), f32),
-            pltpu.VMEM((harms, 2 * kry, 128), f32),
-            pltpu.VMEM((nodes, 8, 128), f32),
-            pltpu.VMEM((harms, 8, 128), f32),
+            pltpu.VMEM((nodes * harms, 1, 128), f32),
+            pltpu.VMEM((nodes * harms, 1, 128), f32),
             pltpu.SemaphoreType.DMA((5,)),
             pltpu.SemaphoreType.DMA((sems,)),
             pltpu.SemaphoreType.DMA((sems,)),
@@ -398,7 +421,7 @@
         ),
         name="arnoldi_step",
     )(neighbours.T, pattern.T, tables, capacity.reshape(1, width), krylov_basis, cond_time, diag_blocks, coupling)
-    norm = norm[0, 0]
+    norm = jnp.sqrt(square[0, 0] + 1e-6)
     return rest * (1.0 / norm), proj, norm
 
 

time: 47.6 us -> 45.4 us (0.954)
  Pallas kernels: 41.6 us -> 39.9 us
  between operations: 2.9 us -> 2.4 us
    pallas_call x1, Pallas kernels: 41.6 us -> 39.9 us  [per_device(): pl.pallas_call(functools.partial(kernel, nodes, harms), out_shape=(jax.Sh...]
where the time goes in v2:
time: 45.4 us; the launch traced here: 45.2 us
  Pallas kernels  39.9 us (88%)
  between operations  2.4 us (5%)
  other arithmetic  1.67 us (4%)
  local copies, waits for them, and re-layouts  1.23 us (3%)
    pallas_call x1, Pallas kernels, per_device(): pl.pallas_call(functools.partial(kernel, nodes, harms), out_shape=(jax.Sh...  39.9 us
    mul x1, other arithmetic, per_device(): return (rest * (1.0 / norm), proj, norm)  1.67 us
    unnamed x1, local copies, waits for them, and re-layouts  1.23 us

profile of v2, /device:TPU:0, one launch (start us, length us, event | category | flops | bytes accessed | tf_op | source)
XLA Modules:
  0.0 45.2 jit_solution(10058494819508314161)
XLA Ops:
  0.6 39.9 %arnoldi_step.1 = (f32[2,16,2048]{2,1,0:T(8,128)}, f32[2,8]{1,0:T(2,128)}, f32[1,1]{1,0:T(1,128)}) custom-call(s32[2,8]{1,0:T(2,128)} %bitcast.5, s32[2,8]{1,0:T(2,128)} %bitcast.6, bf16[2,2,128,128]{3,2,1,0:T(8,128)(2,1)} %constant.7.clone.tables_ref, f32[1,2048]{1,0:T(1,128)} %bitcast.4, f32[8,2,16,2048]{3,2,1,0:T(8,128)} %basis_hbm.1, ...), custom_call_target="tpu_custom_call" | custom-call | tf_op jit(solution)/shard_map/arnoldi_step/pallas_call | solution.py:386
  41.2 1.7 %broadcast_multiply_fusion = f32[2,16,2048]{2,1,0:T(8,128)} fusion(f32[2,16,2048]{2,1,0:T(8,128)} %get-tuple-element.6, f32[]{:T(128)S(6)} %div.3), kind=kLoop, calls=%fused_computation | loop fusion | flops 65536 | bytes 524292 | tf_op jit(solution)/shard_map/mul | solution.py:425
  42.9 1.2 %copy.12 = f32[2,8]{1,0:T(2,128)} copy(f32[2,8]{1,0:T(2,128)} %get-tuple-element.13) | data formatting | bytes 128

commit v3 on v2

--- a/solution.py
+++ b/solution.py
@@ -81,15 +81,16 @@
     total_devices = nodes * harms
     flat = node * harms + harm
 
+    def ahead(me, count):
+        return [me] + [jnp.where(me + step >= count, me + step - count, me + step) for step in range(1, count)]
+
+    node_at, harm_at = ahead(node, nodes), ahead(harm, harms)
+
     def device(step):
-        peer = lax.rem(flat + step, total_devices)
-        return (lax.div(peer, harms), lax.rem(peer, harms))
-
-    def greet(step, carry):
+        return (node_at[step // harms], harm_at[step % harms])
+
+    for step in range(1, total_devices):
         pl.semaphore_signal(barrier, inc=1, device_id=device(step), device_id_type=MESH)
-        return carry
-
-    lax.fori_loop(1, total_devices, greet, 0)
     coupling_tables(node, near_ref, pattern_ref, where_ref, request)
     received[len(OFFSETS), 0] = jnp.zeros((rows, bs), jnp.float32)
     loads[0].wait()
@@ -281,26 +282,20 @@
     def exchange(parts):
         first = reserve(total_devices)
 
-        def copy(step):
-            return pltpu.make_async_remote_copy(
-                src_ref=parts.at[flat],
-                dst_ref=parts.at[flat],
-                send_sem=send_sem.at[first + step],
-                recv_sem=recv_sem.at[first + step],
-                device_id=device(step),
-                device_id_type=MESH,
+        copies = []
+        for step in range(1, total_devices):
+            copies.append(
+                pltpu.make_async_remote_copy(
+                    src_ref=parts.at[flat],
+                    dst_ref=parts.at[flat],
+                    send_sem=send_sem.at[first + step],
+                    recv_sem=recv_sem.at[first + step],
+                    device_id=device(step),
+                    device_id_type=MESH,
+                )
             )
-
-        def start(step, carry):
-            copy(step).start()
-            return carry
-
-        def wait(step, carry):
-            copy(step).wait()
-            return carry
-
-        lax.fori_loop(1, total_devices, start, 0)
-        lax.fori_loop(1, total_devices, wait, 0)
+            copies[-1].start()
+        finish(copies)
         rows = [parts[at] for at in range(total_devices)]
         while len(rows) > 1:
             rows = [sum(rows[at : at + 2][1:], rows[at]) for at in range(0, len(rows), 2)]

time: 45.4 us -> 45.1 us (level)
  no operation moved by 1% of the time
where the time goes in v3:
time: 45.1 us; the launch traced here: 44.9 us
  Pallas kernels  39.6 us (88%)
  between operations  2.4 us (5%)
  other arithmetic  1.67 us (4%)
  local copies, waits for them, and re-layouts  1.23 us (3%)
    pallas_call x1, Pallas kernels, per_device(): pl.pallas_call(functools.partial(kernel, nodes, harms), out_shape=(jax.Sh...  39.6 us
    mul x1, other arithmetic, per_device(): return (rest * (1.0 / norm), proj, norm)  1.67 us
    unnamed x1, local copies, waits for them, and re-layouts  1.23 us

profile of v3, /device:TPU:0, one launch (start us, length us, event | category | flops | bytes accessed | tf_op | source)
XLA Modules:
  0.0 44.9 jit_solution(10649519192678802599)
XLA Ops:
  0.6 39.6 %arnoldi_step.1 = (f32[2,16,2048]{2,1,0:T(8,128)}, f32[2,8]{1,0:T(2,128)}, f32[1,1]{1,0:T(1,128)}) custom-call(s32[2,8]{1,0:T(2,128)} %bitcast.5, s32[2,8]{1,0:T(2,128)} %bitcast.6, bf16[2,2,128,128]{3,2,1,0:T(8,128)(2,1)} %constant.7.clone.tables_ref, f32[1,2048]{1,0:T(1,128)} %bitcast.4, f32[8,2,16,2048]{3,2,1,0:T(8,128)} %basis_hbm.1, ...), custom_call_target="tpu_custom_call" | custom-call | tf_op jit(solution)/shard_map/arnoldi_step/pallas_call | solution.py:381
  40.9 1.7 %broadcast_multiply_fusion = f32[2,16,2048]{2,1,0:T(8,128)} fusion(f32[2,16,2048]{2,1,0:T(8,128)} %get-tuple-element.6, f32[]{:T(128)S(6)} %div.3), kind=kLoop, calls=%fused_computation | loop fusion | flops 65536 | bytes 524292 | tf_op jit(solution)/shard_map/mul | solution.py:420
  42.6 1.2 %copy.12 = f32[2,8]{1,0:T(2,128)} copy(f32[2,8]{1,0:T(2,128)} %get-tuple-element.13) | data formatting | bytes 128
